TPU v7x, 128 devices: a whole 4x4x4 slice. The times are simulated.
128 devices in a mesh: elec: 8 (over y_lo, z), cell: 16 (over y_hi, x, core).
Axes of the slice: x: 4, y: 4 (y_hi: 2, y_lo: 2; y = y_hi * 2 + y_lo), z: 4, core: 2. Of those that a mesh axis runs over, the one named last changes fastest.
Arguments:
- grads: bfloat16 [3, 1024, 2048], P(None, 'elec', 'cell'), may hold values from -6 to 6
- quads: int32 [32768, 4], P('elec'), may hold values from 0 to 1023, all different within a row
- volume: float32 [2048], P('cell'), may hold values from 0.5 to 2
- weight: float32 [32768], P('elec'), may hold values from 0.5 to 2
Outputs:
- hessian: float32 [2048, 2048], P('elec', 'cell')
Inputs may be any that keep to these rules, and one draw needn't show every extreme that they name: `quads`: each row names four different electrodes; every electrode appears in some row.
All inputs are finite; a program needn't handle non-finite values.
Results may differ from a plain program's by a relative error of at most 0.00096.
Values may be sent and summed in bfloat16 or wider, within the bound.
A program may use at most 64 MiB of HBM per device.

v0:
```python
import jax
import jax.numpy as jnp
from jax import lax
from jax.sharding import PartitionSpec as P


def inner_rows(left, right):
    return lax.dot_general(
        left, right, (((0,), (0,)), ((), ())), preferred_element_type=jnp.float32
    )


def per_device(grads, quads, volume, weight):
    measured_rows = quads.shape[0]
    piece = lax.all_gather(grads, "elec", axis=1, tiled=True)
    width = piece.shape[1]
    labels = lax.iota(jnp.int32, width)
    source_map = (
        (quads[:, 0:1] == labels).astype(jnp.float32)
        - (quads[:, 1:2] == labels).astype(jnp.float32)
    ).astype(jnp.bfloat16)
    receive_map = (
        (quads[:, 2:3] == labels).astype(jnp.float32)
        - (quads[:, 3:4] == labels).astype(jnp.float32)
    ).astype(jnp.bfloat16)
    source = jnp.einsum("me,kec->kmc", source_map, piece, preferred_element_type=jnp.float32)
    receiver = jnp.einsum("me,kec->kmc", receive_map, piece, preferred_element_type=jnp.float32)
    source, receiver = (source, receiver)
    dots = source[0] * receiver[0] + source[1] * receiver[1] + source[2] * receiver[2]
    scaled_rows = (weight[:, None] * -(volume[None, :] * dots)).astype(jnp.bfloat16)
    term = inner_rows(lax.all_gather(scaled_rows, "cell", axis=1, tiled=True), scaled_rows)
    summed_rows = lax.psum_scatter(term, "elec", scatter_dimension=0, tiled=True)
    return summed_rows / jnp.float32(measured_rows * lax.axis_size("elec"))


def solution(mesh):
    placed = (P(None, "elec", "cell"), P("elec", None), P("cell"), P("elec"))
    return jax.shard_map(
        per_device, mesh=mesh, in_specs=placed, out_specs=P("elec", "cell"), check_vma=False
    )
```

profile of v0, /device:TPU:12, one launch (start us, length us, event | category | flops | bytes accessed | tf_op | source)
XLA Modules:
  0.0 234.6 jit_solution(18083217160854926386)
XLA Ops:
  6.5 0.0 all-gather.2.cloned.1.call-start
  6.5 1.1 fusion.23
  7.6 30.1 %all_gather.6 = bf16[3,1024,128]{2,1,0:T(8,128)(2,1)S(1)} all-gather(bf16[3,128,128]{2,1,0:T(8,128)(2,1)} %param.4), channel_id=1, replica_groups=mesh['elec'=8,'cell'=16] {'elec'}, dimensions={1}, use_global_device_ids=true | all-gather | bytes 884736 | tf_op jit(solution)/shard_map/all_gather | solution.py:15
  37.7 6.9 %fusion.10 = f32[3,4096,128]{2,1,0:T(8,128)S(1)} fusion(bf16[3,1024,128]{2,1,0:T(8,128)(2,1)S(1)} %all_gather.6, s32[4096]{0:T(1024)S(1)} %bitcast.34, s32[4096]{0:T(1024)S(1)} %bitcast.35), kind=kOutput, calls=%fused_computation.14 | convolution fusion | flops 3246391296 | bytes 7110656 | tf_op jit(solution)/shard_map/me,kec->kmc/dot_general | solution.py:27
  44.6 0.0 copy-start
  44.7 0.0 copy-start.1
  44.7 6.9 %fusion.13 = f32[3,4096,128]{2,1,0:T(8,128)S(1)} fusion(bf16[3,1024,128]{2,1,0:T(8,128)(2,1)S(1)} %all_gather.6, s32[4096]{0:T(1024)S(1)} %bitcast.33, s32[4096]{0:T(1024)S(1)} %bitcast.32), kind=kOutput, calls=%fused_computation.15 | convolution fusion | flops 3246391296 | bytes 7110656 | tf_op jit(solution)/shard_map/me,kec->kmc/dot_general | solution.py:26
  51.6 0.0 copy-done
  51.6 0.0 copy-done.1
  51.6 1.5 fusion.21
  53.2 0.0 all-gather.2.cloned.1.call-update
  53.2 0.0 reduce-scatter.2.cloned.1.call-start
  53.2 121.1 %all-gather.2.cloned.1.call-done = bf16[4096,2048]{1,0:T(8,128)(2,1)} async-done(((bf16[4096,128]{1,0:T(8,128)(2,1)}), bf16[4096,2048]{1,0:T(8,128)(2,1)}) %all-gather.2.cloned.1.call-update) | async-done | bytes 16777232 | tf_op jit(solution)/shard_map/all_gather | solution.py:31
  174.4 11.6 %fusion.24 = f32[2048,128]{1,0:T(8,128)} fusion(bf16[4096,2048]{1,0:T(8,128)(2,1)} %all-gather.2.cloned.1.call-done, bf16[4096,128]{1,0:T(8,128)(2,1)} %fusion.21), kind=kOutput, calls=%fused_computation.28 | convolution fusion | flops 2147483648 | bytes 18874368 | tf_op jit(solution)/shard_map/dot_general | solution.py:8
  186.0 0.0 reduce-scatter.2.cloned.1.call-update
  186.0 40.1 %reduce-scatter.2.cloned.1.call-done = f32[256,128]{1,0:T(8,128)} async-done(((f32[2048,128]{1,0:T(8,128)}), f32[256,128]{1,0:T(8,128)}) %reduce-scatter.2.cloned.1.call-update) | async-done | bytes 131088 | tf_op jit(solution)/shard_map/reduce_scatter | solution.py:32
  226.2 1.6 broadcast_multiply_fusion
Async XLA Ops:
  6.5 167.9 %all-gather.2.cloned.1.call-start = ((), (), s32[]{:S(2)}) async-start(), calls=%async_computation.1 | async-start | bytes 17825792 | tf_op jit(solution)/shard_map/all_gather | solution.py:31
  44.6 7.0 %copy-start = (f32[4096]{0:T(1024)S(1)}, f32[4096]{0:T(1024)}, u32[]{:S(2)}) copy-start(f32[4096]{0:T(1024)} %param.7) | copy-start | bytes 49156
  44.7 7.0 %copy-start.1 = (f32[128]{0:T(128)S(1)}, f32[128]{0:T(128)}, u32[]{:S(2)}) copy-start(f32[128]{0:T(128)} %param.6) | copy-start | bytes 1540
  53.2 173.0 %reduce-scatter.2.cloned.1.call-start = ((), (), s32[]{:S(2)}) async-start(), calls=%async_computation.2 | async-start | bytes 1179648 | tf_op jit(solution)/shard_map/reduce_scatter | solution.py:32
Sparse Core Ops, SparseCore 0:
  53.3 121.0 all-gather.1
  186.1 39.9 reduce-scatter.1
where the time goes:
time: 236 us; the launch traced here: 235 us
  waiting for transfers between devices  161 us (68%)
  blocking collectives  30.1 us (13%)
  matrix products  25.5 us (11%)
  between operations  13.5 us (6%)
  other arithmetic  3.1 us (1%)
    all_gather x1, waiting for transfers between devices, per_device(): lax.all_gather(scaled_rows, 'cell', axis=1, tiled=True)  121 us
    reduce_scatter x1, waiting for transfers between devices, per_device(): lax.psum_scatter(term, 'elec', scatter_dimension=0, tiled=True)  40.1 us
    all_gather x1, blocking collectives, per_device(): piece = lax.all_gather(grads, 'elec', axis=1, tiled=True)  30.1 us
    dot_general x1, matrix products, inner_rows(): lax.dot_general(left, right, (((0,), (0,)), ((), ())), preferred_element_...  11.6 us
    dot_general x1, matrix products, per_device(): jnp.einsum('me,kec->kmc', source_map, piece, preferred_element_type=jnp.f...  6.94 us
    dot_general x1, matrix products, per_device(): jnp.einsum('me,kec->kmc', receive_map, piece, preferred_element_type=jnp....  6.92 us
  transfers between devices with their start and end apart: 2, of which 2 were waited for; matrix products, arithmetic and copies ran while one was open for 0% of the time, Pallas kernels for 0%

commit v1 on v0

v1 whole, which is shorter than its diff:
```python
import functools

import jax
import jax.numpy as jnp
from jax import lax
from jax.experimental import pallas as pl
from jax.experimental.pallas import tpu as pltpu
from jax.sharding import PartitionSpec as P

MESH = pl.DeviceIdType.MESH
NT = (((1,), (1,)), ((), ()))
EARLY = [(0, 0), (0, 1), (1, 0), (2, 0), (3, 0)]
LATE = [(1, 1), (2, 1), (3, 1), (4, 0), (4, 1), (5, 0), (5, 1)]
BLOCKS = EARLY + LATE
STEPS = [(0, 1), (0, 3), (1, 0), (0, 2), (1, 1), (1, 3), (1, 2)]
ROWS = [(0, 0), (0, 1), (0, 2), (1, 0), (1, 0), (1, 0)]
COLS = [(0, 0), (0, 0), (0, 0), (0, 0), (0, 1), (0, 2)]


def dot_nt(left, right):
    return lax.dot_general(left, right, NT, preferred_element_type=jnp.float32)


def kernel(
    g_ref, q_ref, v_ref, w_ref, out_ref,
    gt, vol, vb, ms, mr, a, b, cc, y, v, sums, part, own, strips, fin, dd, tt,
    ready, gs, gr, ps, pr, bs, br, ys, yr, vs, vr, cs, cr, ks, kr, rs, rr, fs, ts, fr, tr,
):
    e = lax.axis_index("elec")
    cell = lax.axis_index("cell")
    ylo, z = e // 4, e % 4
    yhi, x, c = cell // 8, (cell // 2) % 4, cell % 2
    half_x = x // 2
    half_y = yhi

    def at(dy, dx, core):
        return (((yhi + dy) % 2) * 4 + (x + dx) % 4) * 2 + core

    def group(dy, dx):
        return ((yhi + dy) % 2) * 4 + (x + dx) % 4

    def send(src, dst, ssem, rsem, to):
        return pltpu.make_async_remote_copy(
            src, dst, ssem, rsem, device_id=to, device_id_type=MESH
        )

    barrier = pltpu.get_barrier_semaphore()
    for step in range(1, 8):
        pl.semaphore_signal(barrier, inc=1, device_id=((e + step) % 8, cell), device_id_type=MESH)
    for step in range(1, 16):
        pl.semaphore_signal(barrier, inc=1, device_id=(e, (cell + step) % 16), device_id_type=MESH)

    own_columns = pl.ds(pl.multiple_of(e * 128, 128), 128)
    for k in range(3):
        gt[c, pl.ds(k * 128, 128), own_columns] = g_ref[k].T
    vol[c] = jnp.broadcast_to(v_ref[...], (8, 128))
    pl.semaphore_wait(barrier, 22)
    for step in range(1, 16):
        pl.semaphore_signal(ready, inc=1, device_id=(e, (cell + step) % 16), device_id_type=MESH)

    def peer(i):
        dy, dz = STEPS[i]
        return ((ylo + dy) % 2) * 4 + (z + dz) % 4

    def source(i):
        dy, dz = STEPS[i]
        return ((ylo + dy) % 2) * 4 + (z + 4 - dz) % 4

    def piece(electrode_group):
        return gt.at[c, :, pl.ds(pl.multiple_of(electrode_group * 128, 128), 128)]

    partner = (e, at(0, 0, 1 - c))
    gathers = [
        send(piece(e), piece(e), gs.at[i], gr.at[i], (peer(i), cell)) for i in range(7)
    ]
    for copy in gathers:
        copy.start()
    volume_copy = send(vol.at[c], vol.at[c], ps.at[8], pr.at[8], partner)
    volume_copy.start()
    passes = [send(piece(e), piece(e), ps.at[7], pr.at[7], partner)]
    passes[0].start()

    base = pl.multiple_of(c * 2048, 2048)
    electrodes = [q_ref[pl.ds(k, 1), pl.ds(base, 2048)] for k in range(4)]

    def maps(row, carry):
        first = pl.multiple_of(row * 16, 16)
        label = lax.broadcasted_iota(jnp.int32, (16, 2048), 0) + first
        one = jnp.float32(1)
        ms[pl.ds(first, 16), :] = jnp.where(
            label == electrodes[0], one, jnp.where(label == electrodes[1], -one, 0.0)
        ).astype(jnp.bfloat16)
        mr[pl.ds(first, 16), :] = jnp.where(
            label == electrodes[2], one, jnp.where(label == electrodes[3], -one, 0.0)
        ).astype(jnp.bfloat16)
        return carry

    lax.fori_loop(0, 64, maps, 0)
    for i in range(7):
        gathers[i].wait_recv()
        passes.append(send(piece(source(i)), piece(source(i)), ps.at[i], pr.at[i], partner))
        passes[-1].start()
    volume_copy.wait()
    for h in range(2):
        vb[h] = jnp.broadcast_to(vol[h, 0:1, :], (128, 128)).T
    for copy in passes:
        copy.wait_recv()

    to_b = (e, at(0, 3, c))
    to_v = (e, at(0, 1, c))
    to_y = (e, at(1, 0, c))

    def columns(q, width=512):
        return pl.ds(pl.multiple_of(q * width, width), width)

    def b_copy(h, t, q):
        return send(a.at[h, :, columns(q)], b.at[h, :, columns(q)], bs.at[h * 4 + t], br.at[h * 4 + t], to_b)

    def y_copy(h, t, q):
        return send(a.at[h, :, columns(q)], y.at[h, :, columns(q)], ys.at[h * 4 + t], yr.at[h * 4 + t], to_y)

    def v_copy(h, t, q):
        return send(a.at[h, :, columns(q)], v.at[h, :, columns(t)], vs.at[h * 2 + t], vr.at[h * 2 + t], to_v)

    def c_copy(h, t):
        return send(v.at[h, :, columns(t)], cc.at[h, :, columns(t)], cs.at[h * 2 + t], cr.at[h * 2 + t], to_v)

    def chunk(t):
        return (t + 2 * (1 - half_x)) % 4

    def sensitivities(h, t):
        q = chunk(t)
        cols = columns(q)
        source = jnp.dot(gt[h], ms[:, cols], preferred_element_type=jnp.float32)
        receiver = jnp.dot(gt[h], mr[:, cols], preferred_element_type=jnp.float32)
        dots = (
            source[0:128] * receiver[0:128]
            + source[128:256] * receiver[128:256]
            + source[256:384] * receiver[256:384]
        )
        gain = w_ref[:, pl.ds(pl.multiple_of(base + q * 512, 512), 512)]
        volumes = jnp.concatenate([vb[h]] * 4, axis=1)
        a[h, :, cols] = (gain * -(volumes * dots)).astype(jnp.bfloat16)
        if t < 2:
            v_copy(h, t, q).start()
        b_copy(h, t, q).start()
        y_copy(h, t, q).start()

    for t in range(4):
        sensitivities(0, t)
    for t in range(4):
        sensitivities(1, t)
        if t % 2:
            v_copy(0, t // 2, chunk(t // 2)).wait_recv()
            c_copy(0, t // 2).start()

    def put(block, value):
        sums[0, block] = value[:, 0:128]
        sums[1, block] = value[:, 128:256]

    def a_part(half=None):
        if half is None:
            return a[...].reshape(256, 2048)
        return a[:, :, columns(half, 1024)].reshape(256, 1024)

    whole = dot_nt(a_part(), a_part())
    put(0, whole[0:128])
    put(1, whole[128:256])
    for t in range(2):
        v_copy(1, t, chunk(t)).wait_recv()
        c_copy(1, t).start()

    def arrive(h):
        for t in range(4):
            b_copy(h, t, chunk(t)).wait_recv()
            y_copy(h, t, chunk(t)).wait_recv()
        for t in range(2):
            c_copy(h, t).wait_recv()

    def border(h, first):
        put(first, dot_nt(b[h], a_part()))
        put(first + 1, dot_nt(cc[h], a_part(half_x)))
        put(first + 2, dot_nt(y[h, :, columns(half_y, 1024)], a_part(half_y)))

    def core_copy(late):
        blocks = pl.ds(5, 7) if late else pl.ds(0, 5)
        return send(sums.at[1 - c, blocks], part.at[blocks], ks.at[late], kr.at[late], partner)

    def strip_copy(late, i):
        blocks = pl.ds(5, 7) if late else pl.ds(0, 5)
        rows = pl.ds(pl.multiple_of(peer(i) * 16, 16), 16)
        return send(
            own.at[blocks, rows], strips.at[e, blocks],
            rs.at[late * 8 + i], rr.at[late * 8 + i], (peer(i), cell),
        )

    def strip_arrival(late, i):
        blocks = pl.ds(5, 7) if late else pl.ds(0, 5)
        return send(
            own.at[blocks, pl.ds(0, 16)], strips.at[source(i), blocks],
            rs.at[late * 8 + i], rr.at[late * 8 + i], (source(i), cell),
        )

    def add_cores(late):
        core_copy(late).wait()
        for i in range(12):
            if (i >= 5) == bool(late):
                own[i] = sums[c, i] + part[i]

    def scatter(late):
        for i in range(7):
            strip_copy(late, i).start()

    def gather_strips(late):
        first, last = (5, 12) if late else (0, 5)
        rows = pl.ds(pl.multiple_of(e * 16, 16), 16)
        strips[e, first:last] = own[first:last, rows]
        for i in range(7):
            strip_arrival(late, i).wait_recv()
        total = strips[0, first:last]
        for group_of in range(1, 8):
            total = total + strips[group_of, first:last]
        fin[first:last] = total * jnp.float32(1.0 / 32768)

    def deliver(i, start):
        k, r = BLOCKS[i]
        row_half = r
        offset = pl.multiple_of(e * 16, 16)
        landing = dd.at[pl.ds(pl.multiple_of(row_half * 128 + e * 16, 16), 16)]
        row_group, col_group = group(*ROWS[k]), group(*COLS[k])
        copy = send(fin.at[i], landing, fs.at[i], fr, (row_group, col_group * 2 + c))
        if COLS[k] == (0, 0):
            @pl.when(row_group == e)
            def _():
                if start:
                    pltpu.make_async_copy(fin.at[i], landing, fr).start()

            @pl.when(row_group != e)
            def _():
                if start:
                    copy.start()
                else:
                    copy.wait_send()
        elif start:
            copy.start()
        else:
            copy.wait_send()
        if k:
            mirror = send(
                fin.at[i], tt.at[c, pl.ds(offset, 16)], ts.at[i], tr,
                (col_group, row_group * 2 + row_half),
            )
            if start:
                mirror.start()
            else:
                mirror.wait_send()

    arrive(0)
    border(0, 2)
    core_copy(0).start()
    add_cores(0)
    scatter(0)
    gather_strips(0)
    pl.semaphore_wait(ready, 15)
    for i in range(5):
        deliver(i, True)

    arrive(1)
    border(1, 5)
    whole = dot_nt(y[...].reshape(256, 2048), b[...].reshape(256, 2048))
    put(8, whole[0:128])
    put(9, whole[128:256])
    whole = dot_nt(y[:, :, columns(half_x, 1024)].reshape(256, 1024), cc[...].reshape(256, 1024))
    put(10, whole[0:128])
    put(11, whole[128:256])
    core_copy(1).start()
    add_cores(1)
    scatter(1)
    gather_strips(1)
    for i in range(5, 12):
        deliver(i, True)

    for h in range(2):
        for t in range(4):
            b_copy(h, t, chunk(t)).wait_send()
            y_copy(h, t, chunk(t)).wait_send()
        for t in range(2):
            v_copy(h, t, chunk(t)).wait_send()
            c_copy(h, t).wait_send()
    for late in range(2):
        for i in range(7):
            strip_copy(late, i).wait_send()
    for copy in gathers + passes:
        copy.wait_send()


    row_y, row_x = e // 4, e % 4
    dy, dx = (row_y + 2 - yhi) % 2, (row_x + 4 - x) % 4
    kind = dy * 4 + dx
    mirror_only = (kind == 3) | (kind == 5)
    straight_only = (kind == 0) | (kind == 1) | (kind == 7)

    def wait_straight():
        pltpu.make_async_copy(dd, dd, fr).wait()

    def wait_mirror():
        pltpu.make_async_copy(tt, tt, tr).wait()

    @pl.when(mirror_only)
    def _():
        wait_mirror()
        for h in range(2):
            out_ref[pl.ds(h * 128, 128)] = tt[h].T

    @pl.when(straight_only)
    def _():
        wait_straight()
        out_ref[...] = dd[...]

    @pl.when((kind == 2) | (kind == 4) | (kind == 6))
    def _():
        wait_straight()
        wait_mirror()
        for h in range(2):
            out_ref[pl.ds(h * 128, 128)] = dd[pl.ds(h * 128, 128)] + tt[h].T

    for i in range(12):
        deliver(i, False)


def per_device(grads, quads, volume, weight):
    f32, bf16 = jnp.float32, jnp.bfloat16
    dma = pltpu.SemaphoreType.DMA
    vmem = pl.BlockSpec(memory_space=pltpu.VMEM)
    return pl.pallas_call(
        kernel,
        out_shape=jax.ShapeDtypeStruct((256, 128), f32),
        in_specs=[vmem] * 4,
        out_specs=vmem,
        scratch_shapes=[
            pltpu.VMEM((2, 384, 1024), bf16),
            pltpu.VMEM((2, 8, 128), f32),
            pltpu.VMEM((2, 128, 128), f32),
            pltpu.VMEM((1024, 2048), bf16),
            pltpu.VMEM((1024, 2048), bf16),
            pltpu.VMEM((2, 128, 2048), bf16),
            pltpu.VMEM((2, 128, 2048), bf16),
            pltpu.VMEM((2, 128, 1024), bf16),
            pltpu.VMEM((2, 128, 2048), bf16),
            pltpu.VMEM((2, 128, 1024), bf16),
            pltpu.VMEM((2, 12, 128, 128), f32),
            pltpu.VMEM((12, 128, 128), f32),
            pltpu.VMEM((12, 128, 128), f32),
            pltpu.VMEM((8, 12, 16, 128), f32),
            pltpu.VMEM((12, 16, 128), f32),
            pltpu.VMEM((256, 128), f32),
            pltpu.VMEM((2, 128, 128), f32),
            pltpu.SemaphoreType.REGULAR,
            dma((8,)), dma((8,)), dma((9,)), dma((9,)),
            dma((8,)), dma((8,)), dma((8,)), dma((8,)),
            dma((4,)), dma((4,)), dma((4,)), dma((4,)),
            dma((2,)), dma((2,)), dma((16,)), dma((16,)),
            dma((12,)), dma((12,)), dma, dma,
        ],
        compiler_params=pltpu.CompilerParams(
            collective_id=0, has_side_effects=True, vmem_limit_bytes=60000000
        ),
        name="hessian",
    )(grads, quads.T, volume.reshape(1, 128), weight.reshape(1, 4096))


def solution(mesh):
    placed = (P(None, "elec", "cell"), P("elec", None), P("cell"), P("elec"))
    return jax.shard_map(
        per_device, mesh=mesh, in_specs=placed, out_specs=P("elec", "cell"), check_vma=False
    )
```

time: 236 us -> 69.6 us (0.29)
  waiting for transfers between devices: 161 us -> 0 us
  Pallas kernels: 0 us -> 67.5 us
  blocking collectives: 30.1 us -> 0 us
  matrix products: 25.5 us -> 0 us
  between operations: 13.5 us -> 0.01 us
  other arithmetic: 3.1 us -> 0 us
    all_gather x1 -> x0, waiting for transfers between devices: 121 us -> none  [per_device(): lax.all_gather(scaled_rows, 'cell', axis=1, tiled=True)]
    pallas_call x0 -> x1, Pallas kernels: none -> 67.5 us  [per_device(): pl.pallas_call(kernel, out_shape=jax.ShapeDtypeStruct((256, 128), f32), i...]
    reduce_scatter x1 -> x0, waiting for transfers between devices: 40.1 us -> none  [per_device(): lax.psum_scatter(term, 'elec', scatter_dimension=0, tiled=True)]
    all_gather x1 -> x0, blocking collectives: 30.1 us -> none  [per_device(): piece = lax.all_gather(grads, 'elec', axis=1, tiled=True)]
    dot_general x3 -> x0, matrix products: 25.5 us -> none  [the longest x1 11.6 us: inner_rows(): lax.dot_general(left, right, (((0,), (0,)), ((), ())), preferred_element_...]
  transfers between devices with their start and end apart: 2 -> 0, of which waited for: 2 -> 0; matrix products, arithmetic and copies ran while one was open for 0% -> 0% of each run, Pallas kernels for 0% -> 0%
where the time goes in v1:
time: 69.6 us; the launch traced here: 69.1 us
  Pallas kernels  67.5 us (97%)
  local copies, waits for them, and re-layouts  1.57 us (2%)
    pallas_call x1, Pallas kernels, per_device(): pl.pallas_call(kernel, out_shape=jax.ShapeDtypeStruct((256, 128), f32), i...  67.5 us
    unnamed x1, local copies, waits for them, and re-layouts  1.57 us

profile of v1, /device:TPU:12, one launch (start us, length us, event | category | flops | bytes accessed | tf_op | source)
XLA Modules:
  0.0 69.1 jit_solution(2230149978140166523)
XLA Ops:
  0.0 67.5 %hessian.1 = f32[256,128]{1,0:T(8,128)} custom-call(bf16[3,128,128]{2,1,0:T(8,128)(2,1)} %g_ref.1, s32[4,4096]{1,0:T(4,128)} %bitcast.3, f32[1,128]{1,0:T(1,128)} %bitcast.5, f32[1,4096]{1,0:T(1,128)} %bitcast.4), custom_call_target="tpu_custom_call" | custom-call | tf_op jit(solution)/shard_map/hessian/pallas_call | solution.py:335
  67.5 1.6 %copy.6 = f32[256,128]{1,0:T(8,128)} copy(f32[256,128]{1,0:T(8,128)} %hessian.1) | data formatting | bytes 262144

commit v2 on v1

v2 whole, which is shorter than its diff:
```python
import functools

import jax
import jax.numpy as jnp
from jax import lax
from jax.experimental import pallas as pl
from jax.experimental.pallas import tpu as pltpu
from jax.sharding import PartitionSpec as P

MESH = pl.DeviceIdType.MESH
NT = (((1,), (1,)), ((), ()))
EARLY = [(0, 0), (0, 1), (1, 0), (2, 0), (3, 0)]
LATE = [(1, 1), (2, 1), (3, 1), (4, 0), (4, 1), (5, 0), (5, 1)]
BLOCKS = EARLY + LATE
GROUPS = [(0, 5), (5, 5), (10, 2)]
LATER = GROUPS[1:]
STEPS = [(1, 0), (0, 1), (0, 3), (0, 2), (1, 1), (1, 3), (1, 2)]
ROWS = [(0, 0), (0, 1), (0, 2), (1, 0), (1, 0), (1, 0)]
COLS = [(0, 0), (0, 0), (0, 0), (0, 0), (0, 1), (0, 2)]


def dot_nt(left, right):
    return lax.dot_general(left, right, NT, preferred_element_type=jnp.float32)


def kernel(
    g_ref, q_ref, v_ref, w_ref, out_ref,
    gt, vol, vb, ms, mr, a, b, cc, y, v, sums, part, own, strips, fin, dd, tt,
    zparts, zsum, zback, zs, zr, gs, gr, ps, pr, bs, br, ys, yr, vs, vr, cs, cr, ks, kr, rs, rr, fs, ts, fr, tr,
):
    e = lax.axis_index("elec")
    cell = lax.axis_index("cell")
    ylo, z = e // 4, e % 4
    yhi, x, c = cell // 8, (cell // 2) % 4, cell % 2
    half_x = x // 2
    half_y = yhi

    def at(dy, dx, core):
        return (((yhi + dy) % 2) * 4 + (x + dx) % 4) * 2 + core

    def group(dy, dx):
        return ((yhi + dy) % 2) * 4 + (x + dx) % 4

    def send(src, dst, ssem, rsem, to):
        return pltpu.make_async_remote_copy(
            src, dst, ssem, rsem, device_id=to, device_id_type=MESH
        )

    def peer(i):
        dy, dz = STEPS[i]
        return ((ylo + dy) % 2) * 4 + (z + dz) % 4

    def source(i):
        dy, dz = STEPS[i]
        return ((ylo + dy) % 2) * 4 + (z + 4 - dz) % 4

    def piece(group_of):
        return gt.at[c, group_of]

    barrier = pltpu.get_barrier_semaphore()
    partner = (e, at(0, 0, 1 - c))
    near = [(peer(i), cell) for i in range(4)]
    near += [partner, (e, at(0, 1, c)), (e, at(0, 3, c)), (e, at(1, 0, c))]
    for device in near:
        pl.semaphore_signal(barrier, inc=1, device_id=device, device_id_type=MESH)

    for k in range(3):
        gt[c, e, pl.ds(k * 128, 128), :] = g_ref[k].T
    vol[c] = jnp.broadcast_to(v_ref[...], (8, 128))
    pl.semaphore_wait(barrier, len(near))

    def gather_copy(i):
        if i < 4:
            return send(piece(e), piece(e), gs.at[i], gr.at[i], (peer(i), cell))
        there = ylo * 4 + peer(i) % 4
        return send(piece(peer(0)), piece(peer(0)), gs.at[i], gr.at[i], (there, cell))

    def pass_copy(i, core):
        group_of = e if i == 7 else source(i)
        part_of = gt.at[core, group_of]
        return send(part_of, part_of, ps.at[i], pr.at[i], partner)

    def start_gather():
        for i in range(4):
            gather_copy(i).start()
        pass_copy(7, c).start()

    def relay_gather():
        gather_copy(0).wait_recv()
        for i in range(4, 7):
            gather_copy(i).start()

    def pass_on():
        for i in range(7):
            if i:
                gather_copy(i).wait_recv()
            pass_copy(i, c).start()

    def wait_passed():
        for i in range(8):
            pass_copy(i, 1 - c).wait_recv()

    pl.when(c == 0)(start_gather)
    volume_copy = send(vol.at[c], vol.at[c], ps.at[8], pr.at[8], partner)
    volume_copy.start()

    base = pl.multiple_of(c * 2048, 2048)
    electrodes = [q_ref[pl.ds(k, 1), pl.ds(base, 2048)] for k in range(4)]

    def maps(row, carry):
        first = pl.multiple_of(row * 16, 16)
        label = lax.broadcasted_iota(jnp.int32, (16, 2048), 0) + first
        one = jnp.float32(1)
        ms[pl.ds(first, 16), :] = jnp.where(
            label == electrodes[0], one, jnp.where(label == electrodes[1], -one, 0.0)
        ).astype(jnp.bfloat16)
        mr[pl.ds(first, 16), :] = jnp.where(
            label == electrodes[2], one, jnp.where(label == electrodes[3], -one, 0.0)
        ).astype(jnp.bfloat16)
        return carry

    lax.fori_loop(0, 32, maps, 0)
    pl.when(c == 0)(relay_gather)
    lax.fori_loop(32, 64, maps, 0)
    pl.when(c == 1)(start_gather)
    volume_copy.wait()
    for h in range(2):
        vb[h] = jnp.broadcast_to(vol[h, 0:1, :], (128, 128)).T
    pl.when(c == 0)(pass_on)
    pl.when(c == 1)(relay_gather)
    pl.when(c == 1)(wait_passed)

    to_b = (e, at(0, 3, c))
    to_v = (e, at(0, 1, c))
    to_y = (e, at(1, 0, c))

    def columns(q, width=512):
        return pl.ds(pl.multiple_of(q * width, width), width)

    def b_copy(h, q):
        return send(a.at[h, :, columns(q)], b.at[h, :, columns(q)], bs.at[h * 4 + q], br.at[h * 4 + q], to_b)

    def y_copy(h, q):
        return send(a.at[h, :, columns(q)], y.at[h, :, columns(q)], ys.at[h * 4 + q], yr.at[h * 4 + q], to_y)

    def v_copy(h, t, q):
        return send(a.at[h, :, columns(q)], v.at[h, :, columns(t)], vs.at[h * 2 + t], vr.at[h * 2 + t], to_v)

    def c_copy(h, t):
        return send(v.at[h, :, columns(t)], cc.at[h, :, columns(t)], cs.at[h * 2 + t], cr.at[h * 2 + t], to_v)

    def chunk(t):
        return (t + 2 * (1 - half_x)) % 4

    def sensitivities(h, t):
        q = chunk(t)
        cols = columns(q)
        field = jnp.concatenate([gt[h, i] for i in range(8)], axis=1)
        source = jnp.dot(field, ms[:, cols], preferred_element_type=jnp.float32)
        receiver = jnp.dot(field, mr[:, cols], preferred_element_type=jnp.float32)
        dots = (
            source[0:128] * receiver[0:128]
            + source[128:256] * receiver[128:256]
            + source[256:384] * receiver[256:384]
        )
        gain = w_ref[:, pl.ds(pl.multiple_of(base + q * 512, 512), 512)]
        volumes = jnp.concatenate([vb[h]] * 4, axis=1)
        a[h, :, cols] = (gain * -(volumes * dots)).astype(jnp.bfloat16)
        if t < 2 and h == 0:
            v_copy(h, t, q).start()
        if h == 0:
            b_copy(h, q).start()
            y_copy(h, q).start()

    for t in range(4):
        sensitivities(0, t)
    pl.when(c == 1)(pass_on)
    pl.when(c == 0)(wait_passed)
    for t in range(4):
        sensitivities(1, t)
        if t % 2:
            v_copy(0, t // 2, chunk(t // 2)).wait_recv()
            c_copy(0, t // 2).start()

    def put(block, value):
        sums[0, block] = value[:, 0:128]
        sums[1, block] = value[:, 128:256]

    def a_part(half=None):
        if half is None:
            return a[...].reshape(256, 2048)
        return a[:, :, columns(half, 1024)].reshape(256, 1024)

    for t in range(2):
        v_copy(1, t, chunk(t)).start()
    for q in range(4):
        b_copy(1, q).start()
        y_copy(1, q).start()
    whole = dot_nt(a_part(), a_part())
    put(0, whole[0:128])
    put(1, whole[128:256])

    def arrive(h):
        for q in range(4):
            b_copy(h, q).wait_recv()
            y_copy(h, q).wait_recv()
        for t in range(2):
            c_copy(h, t).wait_recv()

    def border(h, first):
        put(first, dot_nt(b[h], a_part()))
        put(first + 1, dot_nt(cc[h], a_part(half_x)))
        put(first + 2, dot_nt(y[h, :, columns(half_y, 1024)], a_part(half_y)))

    def core_copy(group_of):
        first, count = GROUPS[group_of]
        blocks = pl.ds(first, count)
        return send(
            sums.at[1 - c, blocks], part.at[blocks], ks.at[group_of], kr.at[group_of], partner
        )

    def add_cores(group_of):
        core_copy(group_of).wait()
        first, count = GROUPS[group_of]
        for i in range(first, first + count):
            own[i] = (sums[c, i] + part[i]).reshape(2, 4, 16, 128)

    def z_copy(i, receive=False):
        dz = (1, 3, 2)[i]
        there = (z + 4 - dz) % 4 if receive else (z + dz) % 4
        row = there if receive else z
        return send(
            own.at[pl.ds(0, 5), :, there], zparts.at[row], zs.at[i], zr.at[i],
            (ylo * 4 + there, cell),
        )

    def y_fold():
        return send(zsum.at[:, 1 - ylo], zback, zs.at[3], zr.at[3], ((1 - ylo) * 4 + z, cell))

    def fold_early():
        for i in range(3):
            z_copy(i, True).wait_recv()
        total = own[0:5, :, z]
        for i in range(3):
            total = total + zparts[(z + 4 - (1, 3, 2)[i]) % 4]
        zsum[...] = total
        y_fold().start()

    def finish_early():
        y_fold().wait()
        fin[0:5] = (zsum[:, ylo] + zback[...]) * jnp.float32(1.0 / 32768)

    def strip_copy(late, i, receive=False):
        first, count = LATER[late]
        blocks = pl.ds(first, count)
        if receive:
            there, slot = source(i), source(i)
        else:
            there, slot = peer(i), e
        return send(
            own.at[blocks, there // 4, there % 4], strips.at[slot, blocks],
            rs.at[late * 8 + i], rr.at[late * 8 + i], (there, cell),
        )

    def scatter(late):
        for i in range(7):
            strip_copy(late, i).start()

    def gather_strips(late):
        first, count = LATER[late]
        last = first + count
        total = own[first:last, ylo, z]
        for i in range(7):
            strip_copy(late, i, True).wait_recv()
        for i in range(7):
            total = total + strips[source(i), first:last]
        fin[first:last] = total * jnp.float32(1.0 / 32768)

    def deliver(i, start):
        k, r = BLOCKS[i]
        row_half = r
        offset = pl.multiple_of(e * 16, 16)
        landing = dd.at[pl.ds(pl.multiple_of(row_half * 128 + e * 16, 16), 16)]
        row_group, col_group = group(*ROWS[k]), group(*COLS[k])
        copy = send(fin.at[i], landing, fs.at[i], fr, (row_group, col_group * 2 + c))
        if COLS[k] == (0, 0):
            @pl.when(row_group == e)
            def _():
                if start:
                    pltpu.make_async_copy(fin.at[i], landing, fr).start()

            @pl.when(row_group != e)
            def _():
                if start:
                    copy.start()
                else:
                    copy.wait_send()
        elif start:
            copy.start()
        else:
            copy.wait_send()
        if k:
            mirror = send(
                fin.at[i], tt.at[c, pl.ds(offset, 16)], ts.at[i], tr,
                (col_group, row_group * 2 + row_half),
            )
            if start:
                mirror.start()
            else:
                mirror.wait_send()

    arrive(0)
    border(0, 2)
    core_copy(0).start()
    for t in range(2):
        v_copy(1, t, chunk(t)).wait_recv()
        c_copy(1, t).start()
    add_cores(0)
    for i in range(3):
        z_copy(i).start()
    fold_early()

    def halves(ref, half):
        return ref[:, :, columns(half, 1024)].reshape(256, 1024)

    for q in range(2):
        b_copy(1, q).wait_recv()
        y_copy(1, q).wait_recv()
    border_b = dot_nt(b[1, :, 0:1024], a_part(0))
    corner_b = dot_nt(halves(y, 0), halves(b, 0))
    for q in range(2, 4):
        b_copy(1, q).wait_recv()
        y_copy(1, q).wait_recv()
    put(5, border_b + dot_nt(b[1, :, 1024:2048], a_part(1)))
    put(7, dot_nt(y[1, :, columns(half_y, 1024)], a_part(half_y)))
    whole = corner_b + dot_nt(halves(y, 1), halves(b, 1))
    put(8, whole[0:128])
    put(9, whole[128:256])
    for t in range(2):
        c_copy(1, t).wait_recv()
    put(6, dot_nt(cc[1], a_part(half_x)))
    core_copy(1).start()
    whole = dot_nt(halves(y, half_x), cc[...].reshape(256, 1024))
    put(10, whole[0:128])
    put(11, whole[128:256])
    core_copy(2).start()
    add_cores(1)
    scatter(0)
    add_cores(2)
    scatter(1)
    finish_early()
    for i in range(5):
        deliver(i, True)
    gather_strips(0)
    for i in range(5, 10):
        deliver(i, True)
    gather_strips(1)
    for i in range(10, 12):
        deliver(i, True)

    for h in range(2):
        for q in range(4):
            b_copy(h, q).wait_send()
            y_copy(h, q).wait_send()
        for t in range(2):
            v_copy(h, t, chunk(t)).wait_send()
            c_copy(h, t).wait_send()
    for late in range(2):
        for i in range(7):
            strip_copy(late, i).wait_send()
    for i in range(7):
        gather_copy(i).wait_send()
    for i in range(8):
        pass_copy(i, c).wait_send()
    for i in range(3):
        z_copy(i).wait_send()


    row_y, row_x = e // 4, e % 4
    dy, dx = (row_y + 2 - yhi) % 2, (row_x + 4 - x) % 4
    kind = dy * 4 + dx
    mirror_only = (kind == 3) | (kind == 5)
    straight_only = (kind == 0) | (kind == 1) | (kind == 7)

    def wait_straight():
        pltpu.make_async_copy(dd, dd, fr).wait()

    def wait_mirror():
        pltpu.make_async_copy(tt, tt, tr).wait()

    @pl.when(mirror_only)
    def _():
        wait_mirror()
        for h in range(2):
            out_ref[pl.ds(h * 128, 128)] = tt[h].T

    @pl.when(straight_only)
    def _():
        wait_straight()
        out_ref[...] = dd[...]

    @pl.when((kind == 2) | (kind == 4) | (kind == 6))
    def _():
        wait_straight()
        wait_mirror()
        for h in range(2):
            out_ref[pl.ds(h * 128, 128)] = dd[pl.ds(h * 128, 128)] + tt[h].T

    for i in range(12):
        deliver(i, False)


def per_device(grads, quads, volume, weight):
    f32, bf16 = jnp.float32, jnp.bfloat16
    dma = pltpu.SemaphoreType.DMA
    vmem = pl.BlockSpec(memory_space=pltpu.VMEM)
    return pl.pallas_call(
        kernel,
        out_shape=jax.ShapeDtypeStruct((256, 128), f32),
        in_specs=[vmem] * 4,
        out_specs=vmem,
        scratch_shapes=[
            pltpu.VMEM((2, 8, 384, 128), bf16),
            pltpu.VMEM((2, 8, 128), f32),
            pltpu.VMEM((2, 128, 128), f32),
            pltpu.VMEM((1024, 2048), bf16),
            pltpu.VMEM((1024, 2048), bf16),
            pltpu.VMEM((2, 128, 2048), bf16),
            pltpu.VMEM((2, 128, 2048), bf16),
            pltpu.VMEM((2, 128, 1024), bf16),
            pltpu.VMEM((2, 128, 2048), bf16),
            pltpu.VMEM((2, 128, 1024), bf16),
            pltpu.VMEM((2, 12, 128, 128), f32),
            pltpu.VMEM((12, 128, 128), f32),
            pltpu.VMEM((12, 2, 4, 16, 128), f32),
            pltpu.VMEM((8, 12, 16, 128), f32),
            pltpu.VMEM((12, 16, 128), f32),
            pltpu.VMEM((256, 128), f32),
            pltpu.VMEM((2, 128, 128), f32),
            pltpu.VMEM((4, 5, 2, 16, 128), f32),
            pltpu.VMEM((5, 2, 16, 128), f32),
            pltpu.VMEM((5, 16, 128), f32),
            dma((4,)), dma((4,)), dma((8,)), dma((8,)), dma((9,)), dma((9,)),
            dma((8,)), dma((8,)), dma((8,)), dma((8,)),
            dma((4,)), dma((4,)), dma((4,)), dma((4,)),
            dma((3,)), dma((3,)), dma((16,)), dma((16,)),
            dma((12,)), dma((12,)), dma, dma,
        ],
        compiler_params=pltpu.CompilerParams(
            collective_id=0, has_side_effects=True, vmem_limit_bytes=60000000
        ),
        name="hessian",
    )(grads, quads.T, volume.reshape(1, 128), weight.reshape(1, 4096))


def solution(mesh):
    placed = (P(None, "elec", "cell"), P("elec", None), P("cell"), P("elec"))
    return jax.shard_map(
        per_device, mesh=mesh, in_specs=placed, out_specs=P("elec", "cell"), check_vma=False
    )
```

time: 69.6 us -> 65.4 us (0.940)
  Pallas kernels: 67.5 us -> 63.2 us
    pallas_call x1, Pallas kernels: 67.5 us -> 63.2 us  [per_device(): pl.pallas_call(kernel, out_shape=jax.ShapeDtypeStruct((256, 128), f32), i...]
where the time goes in v2:
time: 65.4 us; the launch traced here: 64.8 us
  Pallas kernels  63.2 us (97%)
  local copies, waits for them, and re-layouts  1.57 us (2%)
    pallas_call x1, Pallas kernels, per_device(): pl.pallas_call(kernel, out_shape=jax.ShapeDtypeStruct((256, 128), f32), i...  63.2 us
    unnamed x1, local copies, waits for them, and re-layouts  1.57 us

profile of v2, /device:TPU:12, one launch (start us, length us, event | category | flops | bytes accessed | tf_op | source)
XLA Modules:
  0.0 64.8 jit_solution(5971568617702343682)
XLA Ops:
  0.0 63.2 %hessian.1 = f32[256,128]{1,0:T(8,128)} custom-call(bf16[3,128,128]{2,1,0:T(8,128)(2,1)} %g_ref.1, s32[4,4096]{1,0:T(4,128)} %bitcast.3, f32[1,128]{1,0:T(1,128)} %bitcast.5, f32[1,4096]{1,0:T(1,128)} %bitcast.4), custom_call_target="tpu_custom_call" | custom-call | tf_op jit(solution)/shard_map/hessian/pallas_call | solution.py:417
  63.3 1.6 %copy.6 = f32[256,128]{1,0:T(8,128)} copy(f32[256,128]{1,0:T(8,128)} %hessian.1) | data formatting | bytes 262144

commit v3 on v2

--- a/solution.py
+++ b/solution.py
@@ -24,7 +24,8 @@
 
 
 def kernel(
-    g_ref, q_ref, v_ref, w_ref, out_ref,
+    g_in, q_in, v_in, w_in, out_ref,
+    g_ref, q_ref, v_ref, w_ref, loads,
     gt, vol, vb, ms, mr, a, b, cc, y, v, sums, part, own, strips, fin, dd, tt,
     zparts, zsum, zback, zs, zr, gs, gr, ps, pr, bs, br, ys, yr, vs, vr, cs, cr, ks, kr, rs, rr, fs, ts, fr, tr,
 ):
@@ -54,56 +55,84 @@
         dy, dz = STEPS[i]
         return ((ylo + dy) % 2) * 4 + (z + 4 - dz) % 4
 
-    def piece(group_of):
-        return gt.at[c, group_of]
-
+    def piece(group_of, s):
+        return gt.at[c, group_of, pl.ds(s * 192, 192)]
+
+    arguments = [
+        pltpu.make_async_copy(src, dst, loads.at[i])
+        for i, (src, dst) in enumerate(
+            ((g_in, g_ref), (v_in, v_ref), (q_in, q_ref), (w_in, w_ref))
+        )
+    ]
+    for load in arguments:
+        load.start()
     barrier = pltpu.get_barrier_semaphore()
     partner = (e, at(0, 0, 1 - c))
-    near = [(peer(i), cell) for i in range(4)]
+    near = [(peer(i), cell) for i in range(7)]
     near += [partner, (e, at(0, 1, c)), (e, at(0, 3, c)), (e, at(1, 0, c))]
     for device in near:
         pl.semaphore_signal(barrier, inc=1, device_id=device, device_id_type=MESH)
 
+    for load in arguments[:2]:
+        load.wait()
     for k in range(3):
-        gt[c, e, pl.ds(k * 128, 128), :] = g_ref[k].T
+        turned = g_ref[k].T
+        for s in range(2):
+            gt[c, e, pl.ds(s * 192 + k * 64, 64), :] = turned[s * 64 : s * 64 + 64]
     vol[c] = jnp.broadcast_to(v_ref[...], (8, 128))
     pl.semaphore_wait(barrier, len(near))
 
-    def gather_copy(i):
-        if i < 4:
-            return send(piece(e), piece(e), gs.at[i], gr.at[i], (peer(i), cell))
-        there = ylo * 4 + peer(i) % 4
-        return send(piece(peer(0)), piece(peer(0)), gs.at[i], gr.at[i], (there, cell))
-
-    def pass_copy(i, core):
+    def gather_copy(s, i):
+        if i < 4 or s == 0:
+            group_of, there = e, peer(i)
+        elif i < 6:
+            group_of, there = peer(0), ylo * 4 + peer(i) % 4
+        else:
+            group_of, there = ylo * 4 + (z + 2) % 4, peer(0)
+        part_of = piece(group_of, s)
+        return send(part_of, part_of, gs.at[s * 7 + i], gr.at[s * 7 + i], (there, cell))
+
+    def pass_copy(s, i, core):
         group_of = e if i == 7 else source(i)
-        part_of = gt.at[core, group_of]
-        return send(part_of, part_of, ps.at[i], pr.at[i], partner)
-
-    def start_gather():
-        for i in range(4):
-            gather_copy(i).start()
-        pass_copy(7, c).start()
-
-    def relay_gather():
-        gather_copy(0).wait_recv()
-        for i in range(4, 7):
-            gather_copy(i).start()
-
-    def pass_on():
+        part_of = gt.at[core, group_of, pl.ds(s * 192, 192)]
+        return send(part_of, part_of, ps.at[s * 8 + i], pr.at[s * 8 + i], partner)
+
+    def start_gather(s):
+        for i in range(4 if s else 7):
+            gather_copy(s, i).start()
+        pass_copy(s, 7, c).start()
+
+    def relay_y(s):
+        gather_copy(s, 0).wait_recv()
+        for i in range(4, 6):
+            gather_copy(s, i).start()
+
+    def relay_z(s):
+        gather_copy(s, 3).wait_recv()
+        gather_copy(s, 6).start()
+
+    def pass_on(s):
         for i in range(7):
-            if i:
-                gather_copy(i).wait_recv()
-            pass_copy(i, c).start()
-
-    def wait_passed():
+            if s == 0 or i not in (0, 3):
+                gather_copy(s, i).wait_recv()
+            pass_copy(s, i, c).start()
+
+    def wait_passed(s):
         for i in range(8):
-            pass_copy(i, 1 - c).wait_recv()
-
-    pl.when(c == 0)(start_gather)
-    volume_copy = send(vol.at[c], vol.at[c], ps.at[8], pr.at[8], partner)
+            pass_copy(s, i, 1 - c).wait_recv()
+
+    def on_core(core, *steps):
+        @pl.when(c == core)
+        def _():
+            for step, s in steps:
+                step(s)
+
+    on_core(0, (start_gather, 0))
+    volume_copy = send(vol.at[c], vol.at[c], ps.at[16], pr.at[16], partner)
     volume_copy.start()
 
+    for load in arguments[2:]:
+        load.wait()
     base = pl.multiple_of(c * 2048, 2048)
     electrodes = [q_ref[pl.ds(k, 1), pl.ds(base, 2048)] for k in range(4)]
 
@@ -119,16 +148,18 @@
         ).astype(jnp.bfloat16)
         return carry
 
-    lax.fori_loop(0, 32, maps, 0)
-    pl.when(c == 0)(relay_gather)
-    lax.fori_loop(32, 64, maps, 0)
-    pl.when(c == 1)(start_gather)
+    lax.fori_loop(0, 20, maps, 0)
+    on_core(0, (start_gather, 1))
+    lax.fori_loop(20, 40, maps, 0)
+    on_core(0, (relay_y, 1))
+    lax.fori_loop(40, 64, maps, 0)
+    on_core(1, (start_gather, 0))
     volume_copy.wait()
     for h in range(2):
         vb[h] = jnp.broadcast_to(vol[h, 0:1, :], (128, 128)).T
-    pl.when(c == 0)(pass_on)
-    pl.when(c == 1)(relay_gather)
-    pl.when(c == 1)(wait_passed)
+    on_core(1, (start_gather, 1))
+    on_core(0, (pass_on, 0), (relay_z, 1))
+    on_core(1, (relay_y, 1), (wait_passed, 0))
 
     to_b = (e, at(0, 3, c))
     to_v = (e, at(0, 1, c))
@@ -137,50 +168,75 @@
     def columns(q, width=512):
         return pl.ds(pl.multiple_of(q * width, width), width)
 
-    def b_copy(h, q):
-        return send(a.at[h, :, columns(q)], b.at[h, :, columns(q)], bs.at[h * 4 + q], br.at[h * 4 + q], to_b)
-
-    def y_copy(h, q):
-        return send(a.at[h, :, columns(q)], y.at[h, :, columns(q)], ys.at[h * 4 + q], yr.at[h * 4 + q], to_y)
-
-    def v_copy(h, t, q):
-        return send(a.at[h, :, columns(q)], v.at[h, :, columns(t)], vs.at[h * 2 + t], vr.at[h * 2 + t], to_v)
-
-    def c_copy(h, t):
-        return send(v.at[h, :, columns(t)], cc.at[h, :, columns(t)], cs.at[h * 2 + t], cr.at[h * 2 + t], to_v)
+    def span(h, s):
+        return (pl.ds(s * 64, 64) if h == 0 else pl.ds(0, 128)), (s if h == 0 else 2)
+
+    def b_copy(h, q, s=0):
+        rows, slot = span(h, s)
+        sem = slot * 4 + q
+        return send(a.at[h, rows, columns(q)], b.at[h, rows, columns(q)], bs.at[sem], br.at[sem], to_b)
+
+    def y_copy(h, q, s=0):
+        rows, slot = span(h, s)
+        sem = slot * 4 + q
+        return send(a.at[h, rows, columns(q)], y.at[h, rows, columns(q)], ys.at[sem], yr.at[sem], to_y)
+
+    def v_copy(h, t, q, s=0):
+        rows, slot = span(h, s)
+        sem = slot * 2 + t
+        return send(a.at[h, rows, columns(q)], v.at[h, rows, columns(t)], vs.at[sem], vr.at[sem], to_v)
+
+    def c_copy(h, t, s=0):
+        rows, slot = span(h, s)
+        sem = slot * 2 + t
+        return send(v.at[h, rows, columns(t)], cc.at[h, rows, columns(t)], cs.at[sem], cr.at[sem], to_v)
 
     def chunk(t):
         return (t + 2 * (1 - half_x)) % 4
 
-    def sensitivities(h, t):
+    def sensitivities(h, parts, t):
         q = chunk(t)
         cols = columns(q)
-        field = jnp.concatenate([gt[h, i] for i in range(8)], axis=1)
-        source = jnp.dot(field, ms[:, cols], preferred_element_type=jnp.float32)
-        receiver = jnp.dot(field, mr[:, cols], preferred_element_type=jnp.float32)
-        dots = (
-            source[0:128] * receiver[0:128]
-            + source[128:256] * receiver[128:256]
-            + source[256:384] * receiver[256:384]
-        )
+        first, last = parts[0] * 192, parts[-1] * 192 + 192
+        field = jnp.concatenate([gt[h, i, first:last] for i in range(8)], axis=1)
+        sources = jnp.dot(field, ms[:, cols], preferred_element_type=jnp.float32)
+        receivers = jnp.dot(field, mr[:, cols], preferred_element_type=jnp.float32)
         gain = w_ref[:, pl.ds(pl.multiple_of(base + q * 512, 512), 512)]
-        volumes = jnp.concatenate([vb[h]] * 4, axis=1)
-        a[h, :, cols] = (gain * -(volumes * dots)).astype(jnp.bfloat16)
-        if t < 2 and h == 0:
-            v_copy(h, t, q).start()
-        if h == 0:
-            b_copy(h, q).start()
-            y_copy(h, q).start()
+        for s in parts:
+            low = s * 192 - first
+            dots = (
+                sources[low : low + 64] * receivers[low : low + 64]
+                + sources[low + 64 : low + 128] * receivers[low + 64 : low + 128]
+                + sources[low + 128 : low + 192] * receivers[low + 128 : low + 192]
+            )
+            volumes = jnp.concatenate([vb[h, s * 64 : s * 64 + 64]] * 4, axis=1)
+            a[h, s * 64 : s * 64 + 64, cols] = (gain * -(volumes * dots)).astype(jnp.bfloat16)
+        if h == 0 and t < 2:
+            v_copy(h, t, q, parts[0]).start()
+        b_copy(h, q, parts[0]).start()
+        y_copy(h, q, parts[0]).start()
+
+    def forward(s, t):
+        v_copy(0, t, chunk(t), s).wait_recv()
+        c_copy(0, t, s).start()
 
     for t in range(4):
-        sensitivities(0, t)
-    pl.when(c == 1)(pass_on)
-    pl.when(c == 0)(wait_passed)
+        sensitivities(0, [0], t)
+        if t == 0:
+            on_core(0, (pass_on, 1))
+        if t == 1:
+            on_core(1, (relay_z, 1))
+    on_core(1, (wait_passed, 1))
     for t in range(4):
-        sensitivities(1, t)
+        sensitivities(0, [1], t)
         if t % 2:
-            v_copy(0, t // 2, chunk(t // 2)).wait_recv()
-            c_copy(0, t // 2).start()
+            forward(0, t // 2)
+    on_core(1, (pass_on, 0), (pass_on, 1))
+    on_core(0, (wait_passed, 0), (wait_passed, 1))
+    for t in range(4):
+        sensitivities(1, [0, 1], t)
+        if t % 2:
+            forward(1, t // 2)
 
     def put(block, value):
         sums[0, block] = value[:, 0:128]
@@ -193,19 +249,17 @@
 
     for t in range(2):
         v_copy(1, t, chunk(t)).start()
-    for q in range(4):
-        b_copy(1, q).start()
-        y_copy(1, q).start()
     whole = dot_nt(a_part(), a_part())
     put(0, whole[0:128])
     put(1, whole[128:256])
 
     def arrive(h):
-        for q in range(4):
-            b_copy(h, q).wait_recv()
-            y_copy(h, q).wait_recv()
-        for t in range(2):
-            c_copy(h, t).wait_recv()
+        for s in range(2 - h):
+            for q in range(4):
+                b_copy(h, q, s).wait_recv()
+                y_copy(h, q, s).wait_recv()
+            for t in range(2):
+                c_copy(h, t, s).wait_recv()
 
     def border(h, first):
         put(first, dot_nt(b[h], a_part()))
@@ -358,20 +412,21 @@
     for i in range(10, 12):
         deliver(i, True)
 
-    for h in range(2):
+    for h, s in ((0, 0), (0, 1), (1, 0)):
         for q in range(4):
-            b_copy(h, q).wait_send()
-            y_copy(h, q).wait_send()
+            b_copy(h, q, s).wait_send()
+            y_copy(h, q, s).wait_send()
         for t in range(2):
-            v_copy(h, t, chunk(t)).wait_send()
-            c_copy(h, t).wait_send()
+            v_copy(h, t, chunk(t), s).wait_send()
+            c_copy(h, t, s).wait_send()
     for late in range(2):
         for i in range(7):
             strip_copy(late, i).wait_send()
-    for i in range(7):
-        gather_copy(i).wait_send()
-    for i in range(8):
-        pass_copy(i, c).wait_send()
+    for s in range(2):
+        for i in range(7):
+            gather_copy(s, i).wait_send()
+        for i in range(8):
+            pass_copy(s, i, c).wait_send()
     for i in range(3):
         z_copy(i).wait_send()
 
@@ -416,10 +471,15 @@
     vmem = pl.BlockSpec(memory_space=pltpu.VMEM)
     return pl.pallas_call(
         kernel,
-        out_shape=jax.ShapeDtypeStruct((256, 128), f32),
-        in_specs=[vmem] * 4,
+        out_shape=pltpu.VMEM((256, 128), f32),
+        in_specs=[pl.BlockSpec(memory_space=pl.ANY)] * 4,
         out_specs=vmem,
         scratch_shapes=[
+            pltpu.VMEM((3, 128, 128), bf16),
+            pltpu.VMEM((4, 4096), jnp.int32),
+            pltpu.VMEM((1, 128), f32),
+            pltpu.VMEM((1, 4096), f32),
+            dma((4,)),
             pltpu.VMEM((2, 8, 384, 128), bf16),
             pltpu.VMEM((2, 8, 128), f32),
             pltpu.VMEM((2, 128, 128), f32),
@@ -440,9 +500,9 @@
             pltpu.VMEM((4, 5, 2, 16, 128), f32),
             pltpu.VMEM((5, 2, 16, 128), f32),
             pltpu.VMEM((5, 16, 128), f32),
-            dma((4,)), dma((4,)), dma((8,)), dma((8,)), dma((9,)), dma((9,)),
-            dma((8,)), dma((8,)), dma((8,)), dma((8,)),
-            dma((4,)), dma((4,)), dma((4,)), dma((4,)),
+            dma((4,)), dma((4,)), dma((14,)), dma((14,)), dma((17,)), dma((17,)),
+            dma((12,)), dma((12,)), dma((12,)), dma((12,)),
+            dma((6,)), dma((6,)), dma((6,)), dma((6,)),
             dma((3,)), dma((3,)), dma((16,)), dma((16,)),
             dma((12,)), dma((12,)), dma, dma,
         ],

time: 65.4 us -> 61.5 us (0.940)
  Pallas kernels: 63.2 us -> 60.3 us
  local copies, waits for them, and re-layouts: 1.57 us -> 0.66 us
    pallas_call x1, Pallas kernels: 63.2 us -> 60.3 us  [per_device(): pl.pallas_call(kernel, out_shape=pltpu.VMEM((256, 128), f32), in_specs=[p...]
    unnamed x1, local copies, waits for them, and re-layouts: 1.57 us -> 0.66 us
where the time goes in v3:
time: 61.5 us; the launch traced here: 61 us
  Pallas kernels  60.3 us (98%)
  local copies, waits for them, and re-layouts  0.66 us (1%)
    pallas_call x1, Pallas kernels, per_device(): pl.pallas_call(kernel, out_shape=pltpu.VMEM((256, 128), f32), in_specs=[p...  60.3 us

profile of v3, /device:TPU:12, one launch (start us, length us, event | category | flops | bytes accessed | tf_op | source)
XLA Modules:
  0.0 61.0 jit_solution(2560419699215763211)
XLA Ops:
  0.0 60.3 %hessian.1 = f32[256,128]{1,0:T(8,128)S(1)} custom-call(bf16[3,128,128]{2,1,0:T(8,128)(2,1)} %g_in.1, s32[4,4096]{1,0:T(4,128)} %bitcast.3, f32[1,128]{1,0:T(1,128)} %bitcast.5, f32[1,4096]{1,0:T(1,128)} %bitcast.4), custom_call_target="tpu_custom_call" | custom-call | tf_op jit(solution)/shard_map/hessian/pallas_call | solution.py:472
  60.4 0.7 %copy.6 = f32[256,128]{1,0:T(8,128)} copy(f32[256,128]{1,0:T(8,128)S(1)} %hessian.1) | data formatting | bytes 262144

commit v4 on v3

--- a/solution.py
+++ b/solution.py
@@ -12,7 +12,7 @@
 EARLY = [(0, 0), (0, 1), (1, 0), (2, 0), (3, 0)]
 LATE = [(1, 1), (2, 1), (3, 1), (4, 0), (4, 1), (5, 0), (5, 1)]
 BLOCKS = EARLY + LATE
-GROUPS = [(0, 5), (5, 5), (10, 2)]
+GROUPS = [(0, 5), (5, 3), (8, 2), (10, 2)]
 LATER = GROUPS[1:]
 STEPS = [(1, 0), (0, 1), (0, 3), (0, 2), (1, 1), (1, 3), (1, 2)]
 ROWS = [(0, 0), (0, 1), (0, 2), (1, 0), (1, 0), (1, 0)]
@@ -317,7 +317,7 @@
         )
 
     def scatter(late):
-        for i in range(7):
+        for i in (6, 4, 5, 3, 0, 1, 2):
             strip_copy(late, i).start()
 
     def gather_strips(late):
@@ -387,30 +387,30 @@
         y_copy(1, q).wait_recv()
     put(5, border_b + dot_nt(b[1, :, 1024:2048], a_part(1)))
     put(7, dot_nt(y[1, :, columns(half_y, 1024)], a_part(half_y)))
-    whole = corner_b + dot_nt(halves(y, 1), halves(b, 1))
-    put(8, whole[0:128])
-    put(9, whole[128:256])
     for t in range(2):
         c_copy(1, t).wait_recv()
     put(6, dot_nt(cc[1], a_part(half_x)))
     core_copy(1).start()
+    whole = corner_b + dot_nt(halves(y, 1), halves(b, 1))
+    put(8, whole[0:128])
+    put(9, whole[128:256])
+    core_copy(2).start()
     whole = dot_nt(halves(y, half_x), cc[...].reshape(256, 1024))
     put(10, whole[0:128])
     put(11, whole[128:256])
-    core_copy(2).start()
-    add_cores(1)
-    scatter(0)
-    add_cores(2)
-    scatter(1)
-    finish_early()
-    for i in range(5):
-        deliver(i, True)
-    gather_strips(0)
-    for i in range(5, 10):
-        deliver(i, True)
-    gather_strips(1)
-    for i in range(10, 12):
-        deliver(i, True)
+    core_copy(3).start()
+    for late in range(3):
+        add_cores(late + 1)
+        scatter(late)
+    for late in range(3):
+        gather_strips(late)
+        if late == 0:
+            finish_early()
+            for i in range(5):
+                deliver(i, True)
+        first, count = LATER[late]
+        for i in range(first, first + count):
+            deliver(i, True)
 
     for h, s in ((0, 0), (0, 1), (1, 0)):
         for q in range(4):
@@ -419,7 +419,7 @@
         for t in range(2):
             v_copy(h, t, chunk(t), s).wait_send()
             c_copy(h, t, s).wait_send()
-    for late in range(2):
+    for late in range(3):
         for i in range(7):
             strip_copy(late, i).wait_send()
     for s in range(2):
@@ -503,7 +503,7 @@
             dma((4,)), dma((4,)), dma((14,)), dma((14,)), dma((17,)), dma((17,)),
             dma((12,)), dma((12,)), dma((12,)), dma((12,)),
             dma((6,)), dma((6,)), dma((6,)), dma((6,)),
-            dma((3,)), dma((3,)), dma((16,)), dma((16,)),
+            dma((4,)), dma((4,)), dma((24,)), dma((24,)),
             dma((12,)), dma((12,)), dma, dma,
         ],
         compiler_params=pltpu.CompilerParams(

time: 61.5 us -> 60.6 us (0.985)
  no operation moved by 1% of the time
where the time goes in v4:
time: 60.6 us; the launch traced here: 60.5 us
  Pallas kernels  59.8 us (99%)
  local copies, waits for them, and re-layouts  0.66 us (1%)
    pallas_call x1, Pallas kernels, per_device(): pl.pallas_call(kernel, out_shape=pltpu.VMEM((256, 128), f32), in_specs=[p...  59.8 us

profile of v4, /device:TPU:12, one launch (start us, length us, event | category | flops | bytes accessed | tf_op | source)
XLA Modules:
  0.0 60.5 jit_solution(9433756030453677204)
XLA Ops:
  0.0 59.8 %hessian.1 = f32[256,128]{1,0:T(8,128)S(1)} custom-call(bf16[3,128,128]{2,1,0:T(8,128)(2,1)} %g_in.1, s32[4,4096]{1,0:T(4,128)} %bitcast.3, f32[1,128]{1,0:T(1,128)} %bitcast.5, f32[1,4096]{1,0:T(1,128)} %bitcast.4), custom_call_target="tpu_custom_call" | custom-call | tf_op jit(solution)/shard_map/hessian/pallas_call | solution.py:472
  59.8 0.7 %copy.6 = f32[256,128]{1,0:T(8,128)} copy(f32[256,128]{1,0:T(8,128)S(1)} %hessian.1) | data formatting | bytes 262144

commit v5 on v4

--- a/solution.py
+++ b/solution.py
@@ -337,6 +337,15 @@
         landing = dd.at[pl.ds(pl.multiple_of(row_half * 128 + e * 16, 16), 16)]
         row_group, col_group = group(*ROWS[k]), group(*COLS[k])
         copy = send(fin.at[i], landing, fs.at[i], fr, (row_group, col_group * 2 + c))
+        if k:
+            mirror = send(
+                fin.at[i], tt.at[c, pl.ds(offset, 16)], ts.at[i], tr,
+                (col_group, row_group * 2 + row_half),
+            )
+            if start:
+                mirror.start()
+            else:
+                mirror.wait_send()
         if COLS[k] == (0, 0):
             @pl.when(row_group == e)
             def _():
@@ -353,15 +362,6 @@
             copy.start()
         else:
             copy.wait_send()
-        if k:
-            mirror = send(
-                fin.at[i], tt.at[c, pl.ds(offset, 16)], ts.at[i], tr,
-                (col_group, row_group * 2 + row_half),
-            )
-            if start:
-                mirror.start()
-            else:
-                mirror.wait_send()
 
     arrive(0)
     border(0, 2)

time: 60.6 us -> 60.6 us (level)
  no operation moved by 1% of the time
where the time goes in v5:
time: 60.6 us; the launch traced here: 60.5 us
  Pallas kernels  59.8 us (99%)
  local copies, waits for them, and re-layouts  0.66 us (1%)
    pallas_call x1, Pallas kernels, per_device(): pl.pallas_call(kernel, out_shape=pltpu.VMEM((256, 128), f32), in_specs=[p...  59.8 us

profile of v5, /device:TPU:12, one launch (start us, length us, event | category | flops | bytes accessed | tf_op | source)
XLA Modules:
  0.0 60.5 jit_solution(12747118850367409424)
XLA Ops:
  0.0 59.8 %hessian.1 = f32[256,128]{1,0:T(8,128)S(1)} custom-call(bf16[3,128,128]{2,1,0:T(8,128)(2,1)} %g_in.1, s32[4,4096]{1,0:T(4,128)} %bitcast.3, f32[1,128]{1,0:T(1,128)} %bitcast.5, f32[1,4096]{1,0:T(1,128)} %bitcast.4), custom_call_target="tpu_custom_call" | custom-call | tf_op jit(solution)/shard_map/hessian/pallas_call | solution.py:472
  59.8 0.7 %copy.6 = f32[256,128]{1,0:T(8,128)} copy(f32[256,128]{1,0:T(8,128)S(1)} %hessian.1) | data formatting | bytes 262144
